TPU v7x, 32 devices: a whole 2x2x4 slice. The times are simulated.
32 devices in a mesh: parts: 2 (over x), rows: 16 (over z, y, core).
Axes of the slice: x: 2, y: 2, z: 4, core: 2. Of those that a mesh axis runs over, the one named last changes fastest.
Arguments:
- rhs: float32 [3, 12288, 256], P(None, 'rows', 'parts'), parts along dimension 2, may hold values from -6 to 6
- diag_inv: float32 [3, 12288, 768], P(None, 'rows'), may hold values from -0.21875 to 0.21875
- tiles: float32 [2, 32, 768, 768], P(None, 'rows'), may hold values from -0.15625 to 0.15625
- dest: int32 [2, 16, 2], P(None, 'rows'), may hold values from 0 to 15, all different within a row; in each aligned block of 16 rows (0 to 15, 16 to 31, ..., all dimensions but the last counted through in order) at most 4 rows name the same one
- obs_weight: float32 [12288], P('rows'), may hold values from -0.108253175 to 0.108253175, as said below
Outputs:
- solution: float32 [3, 12288, 256], P(None, 'rows', 'parts'), parts along dimension 2
- observed: float32 [256], P('parts'), parts along dimension 0
There are 2 independent parts, one for each index of `parts`. A program takes and returns all parts, laid end to end along the dimension named above; an argument that names none is the same for every part. Nothing has to cross between parts.
Inputs may be any that keep to these rules, and one draw needn't show every extreme that they name: `dest`: in each of the two levels, the two entries of a supernode differ, and no supernode of the next level is named more than 4 times. `obs_weight`: finite weights.
All inputs are finite; a program needn't handle non-finite values.
Results may differ from a plain program's by a relative error of at most 0.00029.
Values sent between devices are 32-bit elements; how exact they have to be, the bound alone decides.
No kernel may reach another device: no remote copies, remote signals or barrier semaphores. Data moves between devices by JAX's collectives and lax.ppermute only.
A program may use at most 128 MiB of HBM per device.

v0:
```python
import jax
import jax.numpy as jnp
from jax import lax
from jax.sharding import PartitionSpec as P


def collect_updates(solved_block, tiles_level, pattern_level):
    products = jnp.einsum(
        "kab,bc->kac",
        tiles_level,
        solved_block,
        precision=lax.Precision.HIGHEST,
        preferred_element_type=jnp.float32,
    )
    block_rows = solved_block.shape[0]
    width = products.shape[2]
    count = lax.axis_size("rows")
    sliced = lax.all_to_all(products, "rows", split_axis=1, concat_axis=0, tiled=True)
    owners = jnp.arange(count, dtype=jnp.int32)
    flat_targets = pattern_level.reshape(-1)
    matches = (owners[:, None] == flat_targets[None, :]).astype(jnp.float32)
    partial_value = jnp.einsum("mq,qac->mac", matches, sliced, precision=lax.Precision.HIGHEST)
    returned = lax.all_to_all(partial_value, "rows", split_axis=0, concat_axis=0, tiled=True)
    return returned.reshape(block_rows, width)


def body(rhs, diag_inv, tiles, dest, obs_weight):
    pattern = lax.all_gather(dest, "rows", axis=1, tiled=True)
    current = rhs[0]
    solved_levels = []
    solved_block = current
    for section in range(3):
        solved_block = jnp.dot(
            diag_inv[section],
            current,
            precision=lax.Precision.HIGHEST,
            preferred_element_type=jnp.float32,
        )
        solved_levels.append(solved_block)
        if section < 2:
            current = rhs[section + 1] - collect_updates(
                solved_block, tiles[section], pattern[section]
            )
    partial_sum = jnp.dot(
        obs_weight,
        solved_block,
        precision=lax.Precision.HIGHEST,
        preferred_element_type=jnp.float32,
    )
    observed = lax.psum(partial_sum, "rows")
    return (jnp.stack(solved_levels), observed)


def solution(mesh):
    in_specs = (
        P(None, "rows", "parts"),
        P(None, "rows", None),
        P(None, "rows", None, None),
        P(None, "rows", None),
        P("rows"),
    )
    out_specs = (P(None, "rows", "parts"), P("parts"))
    return jax.shard_map(body, mesh=mesh, in_specs=in_specs, out_specs=out_specs, check_vma=False)
```

profile of v0, /device:TPU:0, one launch (start us, length us, event | category | flops | bytes accessed | tf_op | source)
XLA Modules:
  0.0 156.5 jit_solution(14306570408259959369)
XLA Ops:
  0.6 3.7 %fusion.10 = f32[768,128]{1,0:T(8,128)S(1)} fusion(f32[3,768,768]{2,1,0:T(8,128)} %param.6, f32[3,768,128]{2,1,0:T(8,128)} %param.5), kind=kOutput, calls=%fused_computation.10 | convolution fusion | flops 905969664 | bytes 3145728 | tf_op jit(solution)/shard_map/dot_general | solution.py:33
  4.3 7.4 %fusion.15 = f32[2,768,128]{1,2,0:T(8,128)S(1)} fusion(f32[2,2,768,768]{3,2,1,0:T(8,128)} %param.7, f32[768,128]{1,0:T(8,128)S(1)} %fusion.10), kind=kOutput, calls=%fused_computation.15 | convolution fusion | flops 1811939328 | bytes 5898240 | tf_op jit(solution)/shard_map/kab,bc->kac/dot_general | solution.py:8
  11.7 0.0 copy-start.3
  11.7 1.2 copy.23
  12.9 7.5 %all-to-all-start = ((f32[2,768,128]{2,0,1:T(2,128)}), f32[2,768,128]{2,0,1:T(2,128)S(1)}, u32[]{:S(2)}, u32[]{:S(2)}) async-start(f32[2,768,128]{2,0,1:T(2,128)} %copy.23), calls=%async_computation | async-start | bytes 1572864 | tf_op jit(solution)/shard_map/all_to_all | solution.py:18
  20.4 29.2 %all_gather.3 = s32[2,16,2]{2,0,1:T(2,128)S(1)} all-gather(s32[2,1,2]{2,0,1:T(2,128)S(1)} %bitcast.82), channel_id=1, replica_groups=mesh['parts'=2,'rows'=16] {'rows'}, dimensions={1}, use_global_device_ids=true | all-gather | bytes 272 | tf_op jit(solution)/shard_map/all_gather | solution.py:28
  49.7 0.1 eq.31
  49.8 0.0 copy-start
  49.8 0.1 copy.24
  49.8 0.6 copy.25
  50.5 0.4 fusion.29
  50.8 0.1 copy.26
  51.0 16.7 %all_to_all.46 = f32[16,48,128]{2,1,0:T(8,128)S(1)} all-to-all(f32[16,48,128]{2,1,0:T(8,128)S(1)} %copy.26), channel_id=1, replica_groups=mesh['parts'=2,'rows'=16] {'rows'}, dimensions={0} | all-to-all | bytes 786432 | tf_op jit(solution)/shard_map/all_to_all | solution.py:23
  67.7 0.1 bitcast_subtract_fusion.1
  67.8 3.8 %fusion.8 = f32[128,768]{1,0:T(8,128)S(1)} fusion(f32[3,768,768]{2,1,0:T(8,128)} %param.6, f32[1,768,128]{2,1,0:T(8,128)S(1)} %bitcast_subtract_fusion.1), kind=kOutput, calls=%fused_computation.8 | convolution fusion | flops 905969664 | bytes 3145728 | tf_op jit(solution)/shard_map/dot_general | solution.py:33
  71.5 5.0 %fusion.18 = f32[2,768,128]{1,2,0:T(8,128)S(1)} fusion(f32[2,2,768,768]{3,2,1,0:T(8,128)S(1)} %copy-done, f32[128,768]{1,0:T(8,128)S(1)} %fusion.8), kind=kOutput, calls=%fused_computation.16 | convolution fusion | flops 1811939328 | bytes 5898240 | tf_op jit(solution)/shard_map/kab,bc->kac/dot_general | solution.py:8
  76.5 1.2 copy.28
  77.7 3.6 %all-to-all-start.2 = ((f32[2,768,128]{2,0,1:T(2,128)}), f32[2,768,128]{2,0,1:T(2,128)S(1)}, u32[]{:S(2)}, u32[]{:S(2)}) async-start(f32[2,768,128]{2,0,1:T(2,128)} %copy.28), calls=%async_computation.2 | async-start | bytes 1572864 | tf_op jit(solution)/shard_map/all_to_all | solution.py:18
  81.3 0.1 eq.35
  81.4 18.6 %all-to-all-done.2 = f32[2,768,128]{2,0,1:T(2,128)S(1)} async-done(((f32[2,768,128]{2,0,1:T(2,128)}), f32[2,768,128]{2,0,1:T(2,128)S(1)}, u32[]{:S(2)}, u32[]{:S(2)}) %all-to-all-start.2) | async-done | bytes 786464 | tf_op jit(solution)/shard_map/all_to_all | solution.py:18
  99.9 0.1 copy.29
  100.0 0.0 copy-start.2
  100.0 0.6 copy.30
  100.6 0.4 fusion.32
  101.0 0.9 copy.31
  101.9 5.3 %all-to-all-start.3 = ((f32[16,48,128]{2,1,0:T(8,128)}), f32[16,48,128]{2,1,0:T(8,128)S(1)}, u32[]{:S(2)}, u32[]{:S(2)}) async-start(f32[16,48,128]{2,1,0:T(8,128)} %copy.31), calls=%async_computation.3 | async-start | bytes 786432 | tf_op jit(solution)/shard_map/all_to_all | solution.py:23
  107.3 0.2 copy.27
  107.4 12.0 %all-to-all-done.3 = f32[16,48,128]{2,1,0:T(8,128)S(1)} async-done(((f32[16,48,128]{2,1,0:T(8,128)}), f32[16,48,128]{2,1,0:T(8,128)S(1)}, u32[]{:S(2)}, u32[]{:S(2)}) %all-to-all-start.3) | async-done | bytes 393248 | tf_op jit(solution)/shard_map/all_to_all | solution.py:23
  119.4 3.7 %fusion.6 = f32[128,768]{0,1:T(8,128)S(1)} fusion(f32[3,768,768]{2,1,0:T(8,128)} %param.6, f32[1,768,128]{2,1,0:T(8,128)S(1)} %bitcast_subtract_fusion), kind=kOutput, calls=%fused_computation.6 | convolution fusion | flops 905969664 | bytes 3145728 | tf_op jit(solution)/shard_map/dot_general | solution.py:33
  123.1 0.3 convolution_bitcast_fusion
  123.4 32.0 %psum.7 = f32[128]{0:T(128)} all-reduce(f32[128]{0:T(128)S(1)} %convolution_bitcast_fusion), channel_id=1, replica_groups=mesh['parts'=2,'rows'=16] {'rows'}, use_global_device_ids=true, to_apply=%region_0.0 | all-reduce | flops 128 | bytes 1024 | tf_op jit(solution)/shard_map/psum | solution.py:50
  155.4 1.1 pad_maximum_fusion
  (9 shorter events, 0.1 us)
Async XLA Ops:
  11.7 8.7 %copy-start.3 = (s32[2,1,2]{2,1,0:T(1,128)S(1)}, s32[2,1,2]{2,1,0:T(1,128)}, u32[]{:S(2)}) copy-start(s32[2,1,2]{2,1,0:T(1,128)} %param.8) | copy-start | bytes 52
  12.9 54.8 %copy-start.1 = (f32[3,768,128]{2,1,0:T(8,128)S(1)}, f32[3,768,128]{2,1,0:T(8,128)}, u32[]{:S(2)}) copy-start(f32[3,768,128]{2,1,0:T(8,128)} %param.5) | copy-start | bytes 3538948
  12.9 36.9 %all-to-all-start = ((f32[2,768,128]{2,0,1:T(2,128)}), f32[2,768,128]{2,0,1:T(2,128)S(1)}, u32[]{:S(2)}, u32[]{:S(2)}) async-start(f32[2,768,128]{2,0,1:T(2,128)} %copy.23), calls=%async_computation | async-start | bytes 1572864 | tf_op jit(solution)/shard_map/all_to_all | solution.py:18
  49.8 21.8 %copy-start = (f32[2,2,768,768]{3,2,1,0:T(8,128)S(1)}, f32[2,2,768,768]{3,2,1,0:T(8,128)}, u32[]{:S(2)}) copy-start(f32[2,2,768,768]{3,2,1,0:T(8,128)} %param.7) | copy-start | bytes 28311556
  77.7 22.3 %all-to-all-start.2 = ((f32[2,768,128]{2,0,1:T(2,128)}), f32[2,768,128]{2,0,1:T(2,128)S(1)}, u32[]{:S(2)}, u32[]{:S(2)}) async-start(f32[2,768,128]{2,0,1:T(2,128)} %copy.28), calls=%async_computation.2 | async-start | bytes 1572864 | tf_op jit(solution)/shard_map/all_to_all | solution.py:18
  100.0 7.2 %copy-start.2 = (f32[768]{0:T(1024)S(1)}, f32[768]{0:T(1024)}, u32[]{:S(2)}) copy-start(f32[768]{0:T(1024)} %param.9) | copy-start | bytes 9220
  101.9 17.5 %all-to-all-start.3 = ((f32[16,48,128]{2,1,0:T(8,128)}), f32[16,48,128]{2,1,0:T(8,128)S(1)}, u32[]{:S(2)}, u32[]{:S(2)}) async-start(f32[16,48,128]{2,1,0:T(8,128)} %copy.31), calls=%async_computation.3 | async-start | bytes 786432 | tf_op jit(solution)/shard_map/all_to_all | solution.py:23
where the time goes:
time: 157 us
  blocking collectives  77.9 us (50%)
  waiting for transfers between devices  30.5 us (19%)
  matrix products  24.5 us (16%)
  starting transfers between devices  16.5 us (11%)
  local copies, waits for them, and re-layouts  5.05 us (3%)
    psum x1, blocking collectives, body(): observed = lax.psum(partial_sum, 'rows')  32 us
    all_gather x1, blocking collectives, body(): pattern = lax.all_gather(dest, 'rows', axis=1, tiled=True)  29.2 us
    all_to_all x2, waiting for transfers between devices, collect_updates(): lax.all_to_all(products, 'rows', split_axis=1, concat_axis=0, tiled=True)  18.6 us
    all_to_all x1, blocking collectives, collect_updates(): lax.all_to_all(partial_value, 'rows', split_axis=0, concat_axis=0, tiled=...  16.7 us
    dot_general x2, matrix products, collect_updates(): jnp.einsum('kab,bc->kac', tiles_level, solved_block, precision=lax.Precis...  12.3 us
    all_to_all x1, waiting for transfers between devices, collect_updates(): lax.all_to_all(partial_value, 'rows', split_axis=0, concat_axis=0, tiled=...  12 us
    all_to_all x2, starting transfers between devices, collect_updates(): lax.all_to_all(products, 'rows', split_axis=1, concat_axis=0, tiled=True)  11.2 us
    dot_general x3, matrix products, body(): jnp.dot(diag_inv[section], current, precision=lax.Precision.HIGHEST, pref...  11.1 us
  transfers between devices with their start and end apart: 3, of which 2 were waited for; matrix products, arithmetic and copies ran while one was open for 0% of the time, Pallas kernels for 0%

commit v1 on v0

--- a/solution.py
+++ b/solution.py
@@ -2,6 +2,12 @@
 import jax.numpy as jnp
 from jax import lax
 from jax.sharding import PartitionSpec as P
+
+
+def stacked_exchange(shard, axis, split, join):
+    pieces = jnp.split(shard, lax.axis_size(axis), axis=split)
+    incoming = lax.all_to_all(jnp.stack(pieces), axis, 0, 0)
+    return jnp.concatenate(incoming, axis=join)
 
 
 def collect_updates(solved_block, tiles_level, pattern_level):
@@ -15,7 +21,7 @@
     block_rows = solved_block.shape[0]
     width = products.shape[2]
     count = lax.axis_size("rows")
-    sliced = lax.all_to_all(products, "rows", split_axis=1, concat_axis=0, tiled=True)
+    sliced = stacked_exchange(products, "rows", 1, 0)
     owners = jnp.arange(count, dtype=jnp.int32)
     flat_targets = pattern_level.reshape(-1)
     matches = (owners[:, None] == flat_targets[None, :]).astype(jnp.float32)

time: 157 us -> 190 us (1.21)
  local copies, waits for them, and re-layouts: 5.05 us -> 36.3 us
  matrix products: 24.5 us -> 26.7 us
    unnamed x9 -> x53, local copies, waits for them, and re-layouts: 0.03 us -> 19.6 us
    another operation x0 -> x36, local copies, waits for them, and re-layouts: none -> 14 us  [stacked_exchange(): incoming = lax.all_to_all(jnp.stack(pieces), axis, 0, 0)]
    dot_general x2 -> x0, local copies, waits for them, and re-layouts: 2.33 us -> none  [collect_updates(): jnp.einsum('kab,bc->kac', tiles_level, solved_block, precision=lax.Precis...]
    dot_general x2, matrix products: 12.3 us -> 14.5 us  [collect_updates(): jnp.einsum('kab,bc->kac', tiles_level, solved_block, precision=lax.Precis...]
  transfers between devices with their start and end apart: 3 -> 3, of which waited for: 2 -> 2; matrix products, arithmetic and copies ran while one was open for 0% -> 1% of each run, Pallas kernels for 0% -> 0%
where the time goes in v1:
time: 190 us
  blocking collectives  77.6 us (41%)
  local copies, waits for them, and re-layouts  36.3 us (19%)
  waiting for transfers between devices  30.5 us (16%)
  matrix products  26.7 us (14%)
  starting transfers between devices  16.4 us (9%)
    psum x1, blocking collectives, body(): observed = lax.psum(partial_sum, 'rows')  32 us
    all_gather x1, blocking collectives, body(): pattern = lax.all_gather(dest, 'rows', axis=1, tiled=True)  29.2 us
    unnamed x53, local copies, waits for them, and re-layouts  19.6 us
    all_to_all x2, waiting for transfers between devices, stacked_exchange(): incoming = lax.all_to_all(jnp.stack(pieces), axis, 0, 0)  18.5 us
    all_to_all x1, blocking collectives, collect_updates(): lax.all_to_all(partial_value, 'rows', split_axis=0, concat_axis=0, tiled=...  16.4 us
    dot_general x2, matrix products, collect_updates(): jnp.einsum('kab,bc->kac', tiles_level, solved_block, precision=lax.Precis...  14.5 us
    another operation x36, local copies, waits for them, and re-layouts, stacked_exchange(): incoming = lax.all_to_all(jnp.stack(pieces), axis, 0, 0)  14 us
    all_to_all x1, waiting for transfers between devices, collect_updates(): lax.all_to_all(partial_value, 'rows', split_axis=0, concat_axis=0, tiled=...  12 us
  transfers between devices with their start and end apart: 3, of which 2 were waited for; matrix products, arithmetic and copies ran while one was open for 1% of the time, Pallas kernels for 0%

profile of v1, /device:TPU:0, one launch (start us, length us, event | category | flops | bytes accessed | tf_op | source)
XLA Modules:
  0.0 189.7 jit_solution(6801633247055015809)
XLA Ops:
  0.6 3.7 %fusion.10 = f32[768,128]{1,0:T(8,128)S(1)} fusion(f32[3,768,768]{2,1,0:T(8,128)} %param.6, f32[3,768,128]{2,1,0:T(8,128)} %param.5), kind=kOutput, calls=%fused_computation.10 | convolution fusion | flops 905969664 | bytes 3145728 | tf_op jit(solution)/shard_map/dot_general | solution.py:39
  4.3 7.4 %fusion.15 = f32[2,768,128]{1,2,0:T(8,128)S(1)} fusion(f32[2,2,768,768]{3,2,1,0:T(8,128)} %param.7, f32[768,128]{1,0:T(8,128)S(1)} %fusion.10), kind=kOutput, calls=%fused_computation.15 | convolution fusion | flops 1811939328 | bytes 5898240 | tf_op jit(solution)/shard_map/kab,bc->kac/dot_general | solution.py:14
  13.5 0.6 constant_dynamic-update-slice_fusion.15
  23.5 7.4 %all-to-all-start = ((f32[16,2,48,128]{3,2,1,0:T(8,128)}), f32[16,2,48,128]{3,2,1,0:T(8,128)S(1)}, u32[]{:S(2)}, u32[]{:S(2)}) async-start(f32[16,2,48,128]{3,2,1,0:T(8,128)} %constant_dynamic-update-slice_fusion), calls=%async_computation | async-start | bytes 1572864 | tf_op jit(solution)/shard_map/all_to_all | solution.py:9
  31.0 29.2 %all_gather.3 = s32[2,16,2]{2,0,1:T(2,128)S(1)} all-gather(s32[2,1,2]{2,0,1:T(2,128)S(1)} %bitcast.138), channel_id=1, replica_groups=mesh['parts'=2,'rows'=16] {'rows'}, dimensions={1}, use_global_device_ids=true | all-gather | bytes 272 | tf_op jit(solution)/shard_map/all_gather | solution.py:34
  61.8 16.4 %all_to_all.20 = f32[16,48,128]{2,1,0:T(8,128)S(1)} all-to-all(f32[16,48,128]{2,1,0:T(8,128)S(1)} %copy.38), channel_id=1, replica_groups=mesh['parts'=2,'rows'=16] {'rows'}, dimensions={0} | all-to-all | bytes 786432 | tf_op jit(solution)/shard_map/all_to_all | solution.py:29
  78.3 3.8 %fusion.8 = f32[128,768]{1,0:T(8,128)S(1)} fusion(f32[3,768,768]{2,1,0:T(8,128)} %param.6, f32[1,768,128]{2,1,0:T(8,128)S(1)} %bitcast_subtract_fusion.1), kind=kOutput, calls=%fused_computation.8 | convolution fusion | flops 905969664 | bytes 3145728 | tf_op jit(solution)/shard_map/dot_general | solution.py:39
  82.1 7.2 %fusion.18 = f32[2,768,128]{1,2,0:T(8,128)S(1)} fusion(f32[2,2,768,768]{3,2,1,0:T(8,128)} %param.7, f32[128,768]{1,0:T(8,128)S(1)} %fusion.8), kind=kOutput, calls=%fused_computation.16 | convolution fusion | flops 1811939328 | bytes 5898240 | tf_op jit(solution)/shard_map/kab,bc->kac/dot_general | solution.py:14
  89.3 1.3 slice_bitcast_fusion
  90.5 1.6 copy.55
  92.1 1.6 copy.54
  93.7 1.6 copy.53
  95.3 1.6 copy.52
  96.9 0.7 copy.51
  97.6 0.7 copy.50
  98.3 0.7 copy.49
  99.0 0.7 copy.48
  100.3 0.6 constant_dynamic-update-slice_fusion.31
  105.3 1.4 constant_dynamic-update-slice_fusion.23
  106.8 0.6 constant_dynamic-update-slice_fusion.22
  107.4 0.6 constant_dynamic-update-slice_fusion.21
  108.0 0.6 constant_dynamic-update-slice_fusion.20
  108.6 0.6 constant_dynamic-update-slice_fusion.19
  109.3 0.6 constant_dynamic-update-slice_fusion.18
  111.1 3.6 %all-to-all-start.2 = ((f32[16,2,48,128]{3,2,1,0:T(8,128)}), f32[16,2,48,128]{3,2,1,0:T(8,128)S(1)}, u32[]{:S(2)}, u32[]{:S(2)}) async-start(f32[16,2,48,128]{3,2,1,0:T(8,128)} %constant_dynamic-update-slice_fusion.16), calls=%async_computation.2 | async-start | bytes 1572864 | tf_op jit(solution)/shard_map/all_to_all | solution.py:9
  114.9 18.5 %all-to-all-done.2 = f32[16,2,48,128]{3,2,1,0:T(8,128)S(1)} async-done(((f32[16,2,48,128]{3,2,1,0:T(8,128)}), f32[16,2,48,128]{3,2,1,0:T(8,128)S(1)}, u32[]{:S(2)}, u32[]{:S(2)}) %all-to-all-start.2) | async-done | bytes 786464 | tf_op jit(solution)/shard_map/all_to_all | solution.py:9
  134.2 0.9 copy.57
  135.1 5.3 %all-to-all-start.3 = ((f32[16,48,128]{2,1,0:T(8,128)}), f32[16,48,128]{2,1,0:T(8,128)S(1)}, u32[]{:S(2)}, u32[]{:S(2)}) async-start(f32[16,48,128]{2,1,0:T(8,128)} %copy.57), calls=%async_computation.3 | async-start | bytes 786432 | tf_op jit(solution)/shard_map/all_to_all | solution.py:29
  140.6 12.0 %all-to-all-done.3 = f32[16,48,128]{2,1,0:T(8,128)S(1)} async-done(((f32[16,48,128]{2,1,0:T(8,128)}), f32[16,48,128]{2,1,0:T(8,128)S(1)}, u32[]{:S(2)}, u32[]{:S(2)}) %all-to-all-start.3) | async-done | bytes 393248 | tf_op jit(solution)/shard_map/all_to_all | solution.py:29
  152.6 3.7 %fusion.6 = f32[128,768]{0,1:T(8,128)S(1)} fusion(f32[3,768,768]{2,1,0:T(8,128)} %param.6, f32[1,768,128]{2,1,0:T(8,128)S(1)} %bitcast_subtract_fusion), kind=kOutput, calls=%fused_computation.6 | convolution fusion | flops 905969664 | bytes 3145728 | tf_op jit(solution)/shard_map/dot_general | solution.py:39
  156.6 32.0 %psum.7 = f32[128]{0:T(128)} all-reduce(f32[128]{0:T(128)S(1)} %convolution_bitcast_fusion), channel_id=1, replica_groups=mesh['parts'=2,'rows'=16] {'rows'}, use_global_device_ids=true, to_apply=%region_0.0 | all-reduce | flops 128 | bytes 1024 | tf_op jit(solution)/shard_map/psum | solution.py:56
  188.6 1.1 pad_maximum_fusion
  (85 shorter events, 20.4 us)
Async XLA Ops:
  12.8 18.2 %copy-start.10 = (s32[2,1,2]{2,1,0:T(1,128)S(1)}, s32[2,1,2]{2,1,0:T(1,128)}, u32[]{:S(2)}) copy-start(s32[2,1,2]{2,1,0:T(1,128)} %param.8) | copy-start | bytes 52
  23.5 37.3 %all-to-all-start = ((f32[16,2,48,128]{3,2,1,0:T(8,128)}), f32[16,2,48,128]{3,2,1,0:T(8,128)S(1)}, u32[]{:S(2)}, u32[]{:S(2)}) async-start(f32[16,2,48,128]{3,2,1,0:T(8,128)} %constant_dynamic-update-slice_fusion), calls=%async_computation | async-start | bytes 1572864 | tf_op jit(solution)/shard_map/all_to_all | solution.py:9
  30.9 47.3 %copy-start = (f32[3,768,128]{2,1,0:T(8,128)S(1)}, f32[3,768,128]{2,1,0:T(8,128)}, u32[]{:S(2)}) copy-start(f32[3,768,128]{2,1,0:T(8,128)} %param.5) | copy-start | bytes 3538948
  97.6 11.7 %copy-start.3 = (f32[1,2,48,128]{3,2,1,0:T(8,128)S(1)}, f32[1,2,48,128]{3,2,1,0:T(8,128)}, u32[]{:S(2)}) copy-start(f32[1,2,48,128]{3,2,1,0:T(8,128)} %copy.53) | copy-start | bytes 147460
  97.6 12.3 %copy-start.2 = (f32[1,2,48,128]{3,2,1,0:T(8,128)S(1)}, f32[1,2,48,128]{3,2,1,0:T(8,128)}, u32[]{:S(2)}) copy-start(f32[1,2,48,128]{3,2,1,0:T(8,128)} %copy.54) | copy-start | bytes 147460
  97.6 12.9 %copy-start.1 = (f32[1,2,48,128]{3,2,1,0:T(8,128)S(1)}, f32[1,2,48,128]{3,2,1,0:T(8,128)}, u32[]{:S(2)}) copy-start(f32[1,2,48,128]{3,2,1,0:T(8,128)} %copy.55) | copy-start | bytes 147460
  98.3 9.7 %copy-start.5 = (f32[1,2,48,128]{3,2,1,0:T(8,128)S(1)}, f32[1,2,48,128]{3,2,1,0:T(8,128)}, u32[]{:S(2)}) copy-start(f32[1,2,48,128]{3,2,1,0:T(8,128)} %copy.51) | copy-start | bytes 147460
  98.3 10.3 %copy-start.4 = (f32[1,2,48,128]{3,2,1,0:T(8,128)S(1)}, f32[1,2,48,128]{3,2,1,0:T(8,128)}, u32[]{:S(2)}) copy-start(f32[1,2,48,128]{3,2,1,0:T(8,128)} %copy.52) | copy-start | bytes 147460
  99.0 7.8 %copy-start.7 = (f32[1,2,48,128]{3,2,1,0:T(8,128)S(1)}, f32[1,2,48,128]{3,2,1,0:T(8,128)}, u32[]{:S(2)}) copy-start(f32[1,2,48,128]{3,2,1,0:T(8,128)} %copy.49) | copy-start | bytes 147460
  99.0 8.4 %copy-start.6 = (f32[1,2,48,128]{3,2,1,0:T(8,128)S(1)}, f32[1,2,48,128]{3,2,1,0:T(8,128)}, u32[]{:S(2)}) copy-start(f32[1,2,48,128]{3,2,1,0:T(8,128)} %copy.50) | copy-start | bytes 147460
  99.0 15.8 %copy-start.8 = (s32[16,2]{1,0:T(8,128)S(1)}, s32[16,2]{1,0:T(8,128)}, u32[]{:S(2)}) copy-start(s32[16,2]{1,0:T(8,128)} %get-tuple-element.2) | copy-start | bytes 388
  111.1 22.3 %all-to-all-start.2 = ((f32[16,2,48,128]{3,2,1,0:T(8,128)}), f32[16,2,48,128]{3,2,1,0:T(8,128)S(1)}, u32[]{:S(2)}, u32[]{:S(2)}) async-start(f32[16,2,48,128]{3,2,1,0:T(8,128)} %constant_dynamic-update-slice_fusion.16), calls=%async_computation.2 | async-start | bytes 1572864 | tf_op jit(solution)/shard_map/all_to_all | solution.py:9
  114.8 25.6 %copy-start.9 = (f32[768]{0:T(1024)S(1)}, f32[768]{0:T(1024)}, u32[]{:S(2)}) copy-start(f32[768]{0:T(1024)} %param.9) | copy-start | bytes 9220
  135.1 17.5 %all-to-all-start.3 = ((f32[16,48,128]{2,1,0:T(8,128)}), f32[16,48,128]{2,1,0:T(8,128)S(1)}, u32[]{:S(2)}, u32[]{:S(2)}) async-start(f32[16,48,128]{2,1,0:T(8,128)} %copy.57), calls=%async_computation.3 | async-start | bytes 786432 | tf_op jit(solution)/shard_map/all_to_all | solution.py:29
